TPU v7x, 32 devices: a whole 2x2x4 slice. The times are simulated.
32 devices in a mesh: grp: 4 (over y, x), freq: 8 (over z, core).
Axes of the slice: x: 2, y: 2, z: 4, core: 2. Of those that a mesh axis runs over, the one named last changes fastest.
Arguments:
- transfer: bfloat16 [512, 2, 128, 512], P('freq', None, 'grp'), may hold values from -0.1875 to 0.1875
- adjoint: bfloat16 [512, 2, 512, 128], P('freq'), may hold values from -6 to 6
- lower_rows: bfloat16 [131072, 384], P(('grp', 'freq')), may hold values from -6 to 6
- pivot_store: bfloat16 [512, 384], P('grp'), may hold values from -0.3125 to 0.3125
- owners: int32 [3], replicated, may hold values from 0 to 3
- inverse_factor: bfloat16 [128, 128], replicated, as said below
Outputs:
- panel: bfloat16 [131072, 128], P(('grp', 'freq'))
Inputs may be any that keep to these rules, and one draw needn't show every extreme that they name: `inverse_factor`: upper triangular, with diagonal entries from 0.5 to 2.
All inputs are finite; a program needn't handle non-finite values.
Results may differ from a plain program's by a relative error of at most 0.0059.
Values may be sent and summed in bfloat16 or wider, within the bound.
A program may use at most 64 MiB of HBM per device.

v0:
```python
import math

import jax
import jax.numpy as jnp
from jax import lax
from jax.sharding import PartitionSpec as P

C = 128
NF = 512
PANELS = 3
NT = 1024


def make_table(samples, frequencies):
    time_steps = jnp.arange(samples, dtype=jnp.int32)[:, None]
    wave_numbers = jnp.arange(frequencies, dtype=jnp.int32)[None, :]
    phases = (time_steps * wave_numbers % samples).astype(jnp.float32) * (2.0 * math.pi / samples)
    factor = 1.0 / math.sqrt(frequencies)
    return jnp.stack([jnp.cos(phases) * factor, -jnp.sin(phases) * factor]).astype(jnp.bfloat16)


def product(left, right):
    return jnp.einsum("ksm,kmc->ksc", left, right, preferred_element_type=jnp.float32)


def per_device(transfer, adjoint, lower_rows, pivot_store, owners, inverse_factor):
    trans_real = transfer[:, 0]
    trans_imag = transfer[:, 1]
    adjoint_real = adjoint[:, 0]
    adjoint_imag = adjoint[:, 1]
    real_part = product(trans_real, adjoint_real) - product(trans_imag, adjoint_imag)
    imag_part = product(trans_real, adjoint_imag) + product(trans_imag, adjoint_real)
    spectra = jnp.stack([real_part, imag_part], axis=2).astype(jnp.bfloat16)
    table = make_table(NT, NF)
    hessian = jnp.einsum(
        "qtk,ksqc->stc",
        table,
        lax.all_to_all(spectra, "freq", split_axis=1, concat_axis=0, tiled=True),
        preferred_element_type=jnp.float32,
    )
    hessian = hessian.reshape(-1, hessian.shape[-1])
    owned_mask = (owners == lax.axis_index("grp")).astype(jnp.float32)
    local_blocks = pivot_store.reshape(C, PANELS, C).astype(jnp.float32) * owned_mask[None, :, None]
    combined = lax.psum(local_blocks.astype(jnp.bfloat16), "grp")
    pivots = combined.reshape(C, PANELS * C)
    update = lax.dot_general(
        lower_rows, pivots, (((1,), (1,)), ((), ())), preferred_element_type=jnp.float32
    )
    reduced = (hessian - update).astype(jnp.bfloat16)
    return jnp.dot(reduced, inverse_factor, preferred_element_type=jnp.float32).astype(jnp.bfloat16)


def solution(mesh):
    in_specs = (
        P("freq", None, "grp", None),
        P("freq", None, None, None),
        P(("grp", "freq"), None),
        P("grp", None),
        P(),
        P(),
    )
    out_specs = P(("grp", "freq"), None)
    return jax.shard_map(
        per_device, mesh=mesh, in_specs=in_specs, out_specs=out_specs, check_vma=False
    )
```

profile of v0, /device:TPU:0, one launch (start us, length us, event | category | flops | bytes accessed | tf_op | source)
XLA Modules:
  0.0 87.9 jit_solution(477097812663604727)
XLA Ops:
  6.5 5.5 %fusion.2 = f32[64,32,128]{2,1,0:T(8,128)S(1)} fusion(bf16[64,2,512,128]{3,2,1,0:T(8,128)(2,1)} %param.7, bf16[64,2,32,512]{3,2,1,0:T(8,128)(2,1)} %param.6), kind=kOutput, calls=%fused_computation.2 | convolution fusion | flops 268435456 | bytes 11534336 | tf_op jit(solution)/shard_map/ksm,kmc->ksc/dot_general | solution.py:23
  12.0 5.5 %fusion = f32[64,32,128]{2,1,0:T(8,128)S(1)} fusion(bf16[64,2,512,128]{3,2,1,0:T(8,128)(2,1)} %param.7, bf16[64,2,32,512]{3,2,1,0:T(8,128)(2,1)S(1)} %copy-done.6), kind=kOutput, calls=%fused_computation | convolution fusion | flops 268435456 | bytes 11534336 | tf_op jit(solution)/shard_map/ksm,kmc->ksc/dot_general | solution.py:23
  17.6 1.5 %copy-done.5 = bf16[64,2,512,128]{3,2,1,0:T(8,128)(2,1)S(1)} copy-done((bf16[64,2,512,128]{3,2,1,0:T(8,128)(2,1)S(1)}, bf16[64,2,512,128]{3,2,1,0:T(8,128)(2,1)}, u32[]{:S(2)}) %copy-start.5) | copy-done | bytes 16777240
  19.1 1.4 %fusion.52 = bf16[64,32,1,128]{3,1,0,2:T(8,128)(2,1)S(1)} fusion(f32[64,32,128]{2,1,0:T(8,128)S(1)} %fusion.2, bf16[64,2,512,128]{3,2,1,0:T(8,128)(2,1)S(1)} %copy-done.5, bf16[64,2,32,512]{3,2,1,0:T(8,128)(2,1)S(1)} %copy-done.6), kind=kOutput, calls=%fused_computation.44 | convolution fusion | flops 268959744 | bytes 12058624 | tf_op jit(solution)/shard_map/ksm,kmc->ksc/dot_general | solution.py:23
  20.5 1.4 %fusion.57 = bf16[64,32,1,128]{3,1,0,2:T(8,128)(2,1)S(1)} fusion(f32[64,32,128]{2,1,0:T(8,128)S(1)} %fusion, bf16[64,2,512,128]{3,2,1,0:T(8,128)(2,1)S(1)} %copy-done.5, bf16[64,2,32,512]{3,2,1,0:T(8,128)(2,1)S(1)} %copy-done.6), kind=kOutput, calls=%fused_computation.45 | convolution fusion | flops 268959744 | bytes 12058624 | tf_op jit(solution)/shard_map/ksm,kmc->ksc/dot_general | solution.py:23
  21.9 0.1 pad_maximum_fusion
  22.0 0.0 copy-start.3
  22.0 0.0 copy-start.7
  22.0 1.4 %copy.33 = bf16[64,32,2,128]{3,0,2,1:T(8,128)(2,1)} copy(bf16[64,32,2,128]{3,1,0,2:T(8,128)(2,1)S(1)} %pad_maximum_fusion) | data formatting | bytes 2097152 | tf_op jit(solution)/shard_map/stack | solution.py:33
  23.4 6.4 %all-to-all-start = ((bf16[64,32,2,128]{3,0,2,1:T(8,128)(2,1)}), bf16[64,32,2,128]{3,0,2,1:T(8,128)(2,1)}, u32[]{:S(2)}, u32[]{:S(2)}) async-start(bf16[64,32,2,128]{3,0,2,1:T(8,128)(2,1)} %copy.33), calls=%async_computation | async-start | bytes 2097152 | tf_op jit(solution)/shard_map/all_to_all | solution.py:38
  29.7 0.0 all-reduce.2.cloned.1.call-start
  29.8 0.1 copy.37
  29.9 0.7 fusion.62
  30.7 0.0 all-reduce.2.cloned.1.call-update
  30.7 9.3 %multiply_convert_fusion = (bf16[1,1024,512]{2,1,0:T(8,128)(2,1)}, bf16[1,1024,512]{2,1,0:T(8,128)(2,1)}) fusion(), kind=kLoop, calls=%fused_computation.30 | loop fusion | flops 9961472 | bytes 2097152 | tf_op jit(solution)/shard_map/convert.2
  40.0 16.4 %all-to-all-done = bf16[64,32,2,128]{3,0,2,1:T(8,128)(2,1)} async-done(((bf16[64,32,2,128]{3,0,2,1:T(8,128)(2,1)}), bf16[64,32,2,128]{3,0,2,1:T(8,128)(2,1)}, u32[]{:S(2)}, u32[]{:S(2)}) %all-to-all-start) | async-done | bytes 1048608 | tf_op jit(solution)/shard_map/all_to_all | solution.py:38
  56.4 1.4 %copy.34 = bf16[8,64,4,2,128]{4,1,0,3,2:T(8,128)(2,1)S(1)} copy(bf16[8,64,4,2,128]{4,1,3,2,0:T(8,128)(2,1)} %bitcast.7) | data formatting | bytes 2097152 | tf_op jit(solution)/shard_map/all_to_all | solution.py:38
  57.9 0.1 copy-done.1
  57.9 0.3 copy-done.2
  58.3 2.6 %fusion.31 = f32[4,1024,128]{1,2,0:T(8,128)} fusion(bf16[512,4,2,128]{3,0,2,1:T(8,128)(2,1)S(1)} %bitcast.87, bf16[1,1024,512]{2,1,0:T(8,128)(2,1)S(1)} %copy-done.1, bf16[1,1024,512]{2,1,0:T(8,128)(2,1)S(1)} %copy-done.2), kind=kOutput, calls=%fused_computation.39 | convolution fusion | flops 1074790400 | bytes 5242880 | tf_op jit(solution)/shard_map/qtk,ksqc->stc/dot_general | solution.py:35
  60.9 2.9 %copy.36 = f32[4,1024,128]{2,1,0:T(8,128)} copy(f32[4,1024,128]{1,2,0:T(8,128)} %fusion.31) | data formatting | bytes 4194304 | tf_op jit(solution)/shard_map/qtk,ksqc->stc/transpose | solution.py:35
  63.8 2.9 %copy.38 = f32[4096,128]{0,1:T(8,128)} copy(f32[4096,128]{1,0:T(8,128)} %bitcast.86) | data formatting | bytes 4194304 | tf_op jit(solution)/shard_map/reshape | solution.py:41
  66.7 10.3 %all-reduce.2.cloned.1.call-done = bf16[128,384]{0,1:T(8,128)(2,1)} async-done(((bf16[128,384]{0,1:T(8,128)(2,1)}), bf16[128,384]{0,1:T(8,128)(2,1)}) %all-reduce.2.cloned.1.call-update) | async-done | bytes 98320 | tf_op jit(solution)/shard_map/psum | solution.py:44
  77.0 4.1 %convolution_convert_fusion = bf16[4096,128]{1,0:T(8,128)(2,1)} fusion(bf16[128,128]{1,0:T(8,128)(2,1)S(1)} %copy-done.4, f32[4096,128]{0,1:T(8,128)} %copy.38, bf16[128,384]{0,1:T(8,128)(2,1)} %all-reduce.2.cloned.1.call-done, bf16[4096,384]{1,0:T(8,128)(2,1)S(1)} %copy-done), kind=kOutput, calls=%fused_computation.15 | convolution fusion | flops 538443776 | bytes 6422528 | tf_op jit(solution)/shard_map/dot_general | solution.py:50
  (12 shorter events, 0.0 us)
Async XLA Ops:
  6.5 70.5 %copy-start = (bf16[4096,384]{1,0:T(8,128)(2,1)S(1)}, bf16[4096,384]{1,0:T(8,128)(2,1)}, u32[]{:S(2)}) copy-start(bf16[4096,384]{1,0:T(8,128)(2,1)} %param.8) | copy-start | bytes 9437188
  6.5 5.5 %copy-start.6 = (bf16[64,2,32,512]{3,2,1,0:T(8,128)(2,1)S(1)}, bf16[64,2,32,512]{3,2,1,0:T(8,128)(2,1)}, u32[]{:S(2)}) copy-start(bf16[64,2,32,512]{3,2,1,0:T(8,128)(2,1)} %param.6) | copy-start | bytes 12582916
  6.5 12.6 %copy-start.5 = (bf16[64,2,512,128]{3,2,1,0:T(8,128)(2,1)S(1)}, bf16[64,2,512,128]{3,2,1,0:T(8,128)(2,1)}, u32[]{:S(2)}) copy-start(bf16[64,2,512,128]{3,2,1,0:T(8,128)(2,1)} %param.7) | copy-start | bytes 50331652
  22.0 7.8 %copy-start.3 = (bf16[128,384]{1,0:T(8,128)(2,1)S(1)}, bf16[128,384]{1,0:T(8,128)(2,1)}, u32[]{:S(2)}) copy-start(bf16[128,384]{1,0:T(8,128)(2,1)} %param.9) | copy-start | bytes 294916
  22.0 7.9 %copy-start.7 = (s32[3]{0:T(128)S(1)}, s32[3]{0:T(128)}, u32[]{:S(2)}) copy-start(s32[3]{0:T(128)} %param.10) | copy-start | bytes 40
  23.4 33.0 %all-to-all-start = ((bf16[64,32,2,128]{3,0,2,1:T(8,128)(2,1)}), bf16[64,32,2,128]{3,0,2,1:T(8,128)(2,1)}, u32[]{:S(2)}, u32[]{:S(2)}) async-start(bf16[64,32,2,128]{3,0,2,1:T(8,128)(2,1)} %copy.33), calls=%async_computation | async-start | bytes 2097152 | tf_op jit(solution)/shard_map/all_to_all | solution.py:38
  29.7 47.3 %all-reduce.2.cloned.1.call-start = ((), (), s32[]{:S(2)}) async-start(), calls=%async_computation.1 | async-start | bytes 196608 | tf_op jit(solution)/shard_map/psum | solution.py:44
  56.4 1.5 %copy-start.1 = (bf16[1,1024,512]{2,1,0:T(8,128)(2,1)S(1)}, bf16[1,1024,512]{2,1,0:T(8,128)(2,1)}, u32[]{:S(2)}) copy-start(bf16[1,1024,512]{2,1,0:T(8,128)(2,1)} %get-tuple-element.5) | copy-start | bytes 3145732
  56.4 1.9 %copy-start.2 = (bf16[1,1024,512]{2,1,0:T(8,128)(2,1)S(1)}, bf16[1,1024,512]{2,1,0:T(8,128)(2,1)}, u32[]{:S(2)}) copy-start(bf16[1,1024,512]{2,1,0:T(8,128)(2,1)} %get-tuple-element.6) | copy-start | bytes 3145732
  63.8 13.2 %copy-start.4 = (bf16[128,128]{1,0:T(8,128)(2,1)S(1)}, bf16[128,128]{1,0:T(8,128)(2,1)}, u32[]{:S(2)}) copy-start(bf16[128,128]{1,0:T(8,128)(2,1)} %param.11) | copy-start | bytes 98308
Sparse Core Ops, SparseCore 0:
  33.4 43.5 all-reduce.1
where the time goes:
time: 88.2 us; the launch traced here: 87.9 us
  waiting for transfers between devices  26.7 us (30%)
  matrix products  20.4 us (23%)
  between operations  13.5 us (15%)
  local copies, waits for them, and re-layouts  10.7 us (12%)
  other arithmetic  10.2 us (12%)
  starting transfers between devices  6.39 us (7%)
    all_to_all x1, waiting for transfers between devices, per_device(): lax.all_to_all(spectra, 'freq', split_axis=1, concat_axis=0, tiled=True)  16.4 us
    dot_general x4, matrix products, product(): jnp.einsum('ksm,kmc->ksc', left, right, preferred_element_type=jnp.float32)  13.8 us
    psum x1, waiting for transfers between devices, per_device(): combined = lax.psum(local_blocks.astype(jnp.bfloat16), 'grp')  10.3 us
    another operation x1, other arithmetic  9.32 us
    all_to_all x1, starting transfers between devices, per_device(): lax.all_to_all(spectra, 'freq', split_axis=1, concat_axis=0, tiled=True)  6.35 us
    dot_general x1, matrix products, per_device(): jnp.dot(reduced, inverse_factor, preferred_element_type=jnp.float32)  4.05 us
    transpose x1, local copies, waits for them, and re-layouts, per_device(): jnp.einsum('qtk,ksqc->stc', table, lax.all_to_all(spectra, 'freq', split_...  2.91 us
    reshape x1, local copies, waits for them, and re-layouts, per_device(): hessian = hessian.reshape(-1, hessian.shape[-1])  2.91 us
  transfers between devices with their start and end apart: 2, of which 2 were waited for; matrix products, arithmetic and copies ran while one was open for 23% of the time, Pallas kernels for 0%

commit v1 on v0

v1 whole, which is shorter than its diff:
```python
import functools
import math

import jax
import jax.numpy as jnp
from jax import lax
from jax.experimental import pallas as pl
from jax.experimental.pallas import tpu as pltpu
from jax.sharding import PartitionSpec as P

MESH = pl.DeviceIdType.MESH
CHUNK = 8
AHEAD = 3
COARSE = 32


def flip(me, mask):
    bit = 1
    other = me
    while bit <= mask:
        if mask & bit:
            other = other + bit * (1 - 2 * lax.rem(me // bit, 2))
        bit *= 2
    return other


def kernel(
    nf, ng, kc,
    owners_ref, tr_hbm, ad_hbm, lo_hbm, pv_hbm, out_ref,
    tr, ad, lo, pv, spec, sbuf, rbuf, table, acc,
    in_sem, lo_sem, pv_sem, own_sem, send_sem, recv_sem, psend_sem, precv_sem,
):
    kl, _, sl, _ = tr.shape
    c = ad.shape[3]
    nch = kl // kc
    s_loc = sl // nf
    nt, width = acc.shape
    me = lax.axis_index("freq")
    grp = lax.axis_index("grp")

    barrier = pltpu.get_barrier_semaphore()
    for mask in range(1, nf):
        pl.semaphore_signal(barrier, inc=1, device_id={"freq": flip(me, mask)}, device_id_type=MESH)
    for mask in range(1, ng):
        pl.semaphore_signal(barrier, inc=1, device_id={"grp": flip(grp, mask)}, device_id_type=MESH)

    def loads(j):
        rows = pl.ds(j * kc, kc)
        return (
            pltpu.make_async_copy(tr_hbm.at[rows], tr.at[rows], in_sem.at[j, 0]),
            pltpu.make_async_copy(ad_hbm.at[rows], ad.at[rows], in_sem.at[j, 1]),
        )

    lo_copy = pltpu.make_async_copy(lo_hbm, lo, lo_sem)
    pv_copy = pltpu.make_async_copy(pv_hbm, pv.at[grp], pv_sem)

    for j in range(min(AHEAD, nch)):
        for copy in loads(j):
            copy.start()

    def spectra(j):
        for copy in loads(j):
            copy.wait()
        for i in range(kc):
            k = j * kc + i
            right = jnp.concatenate([ad[k, 0], ad[k, 1]], axis=1)
            left = jnp.concatenate([tr[k, 0], tr[k, 1]], axis=0)
            both = jnp.dot(left, right, preferred_element_type=jnp.float32)
            spec[0, pl.ds(i * sl, sl), :] = both[:sl, :c] - both[sl:, c:]
            spec[1, pl.ds(i * sl, sl), :] = both[:sl, c:] + both[sl:, :c]
        for d in range(nf):
            for s in range(s_loc):
                rows = pl.ds(d * s_loc + s, kc, stride=sl)
                block = jnp.concatenate([spec[0, rows, :], spec[1, rows, :]], axis=0)
                sbuf[j, d, :, s * c:(s + 1) * c] = block.astype(jnp.bfloat16)

    def own_copy(j):
        return pltpu.make_async_copy(sbuf.at[j, me], rbuf.at[j, me], own_sem.at[j])

    def remote(j, mask):
        return pltpu.make_async_remote_copy(
            src_ref=sbuf.at[j, flip(me, mask)],
            dst_ref=rbuf.at[j, me],
            send_sem=send_sem.at[j, mask],
            recv_sem=recv_sem.at[j, mask],
            device_id={"freq": flip(me, mask)},
            device_id_type=MESH,
        )

    def arrival(j, mask):
        other = flip(me, mask)
        return pltpu.make_async_remote_copy(
            src_ref=sbuf.at[j, other],
            dst_ref=rbuf.at[j, other],
            send_sem=send_sem.at[j, mask],
            recv_sem=recv_sem.at[j, mask],
            device_id={"freq": other},
            device_id_type=MESH,
        )

    def pivot_copy(mask, slot):
        return pltpu.make_async_remote_copy(
            src_ref=pv_hbm,
            dst_ref=pv.at[slot],
            send_sem=psend_sem.at[mask],
            recv_sem=precv_sem.at[mask],
            device_id={"grp": flip(grp, mask)},
            device_id_type=MESH,
        )

    def send(j):
        for mask in range(nf - 1, 0, -1):
            remote(j, mask).start()
        own_copy(j).start()

    spectra(0)
    pl.semaphore_wait(barrier, nf - 1 + ng - 1)
    send(0)

    @pl.loop(1, nch)
    def _(j):
        @pl.when(j + AHEAD - 1 < nch)
        def _():
            for copy in loads(j + AHEAD - 1):
                copy.start()

        spectra(j)
        send(j)

    pv_copy.start()
    lo_copy.start()
    for mask in range(1, ng):
        pivot_copy(mask, grp).start()

    cols = nf * 2 * kc
    coarse = nt // COARSE
    scale = 1.0 / math.sqrt(kl * nf)
    turn = 2.0 * math.pi / nt

    @pl.loop(0, nch)
    def _(j):
        def phase(rows, step, shift):
            col = lax.broadcasted_iota(jnp.int32, (rows, cols), 1)
            row = lax.broadcasted_iota(jnp.int32, (rows, cols), 0) * step
            kk = (col // (2 * kc)) * kl + j * kc + col % kc
            q = (col // kc) % 2
            whole = kk * row + q * shift
            return (whole % nt).astype(jnp.float32) * turn

        high = phase(coarse, COARSE, 0)
        low = phase(COARSE, 1, nt // 4)
        cos_high, sin_high = jnp.cos(high) * scale, jnp.sin(high) * scale
        cos_low, sin_low = jnp.cos(low), jnp.sin(low)
        for a in range(coarse):
            value = cos_high[a:a + 1] * cos_low - sin_high[a:a + 1] * sin_low
            table[j, a * COARSE:(a + 1) * COARSE, :] = value.astype(jnp.bfloat16)

    lo_copy.wait()
    pv_copy.wait()
    for mask in range(1, ng):
        pivot_copy(mask, flip(grp, mask)).wait_recv()
    panels = lo.shape[1] // c
    pivots = jnp.concatenate(
        [pv[owners_ref[p], :, p * c:(p + 1) * c] for p in range(panels)], axis=1
    )
    tile = min(256, nt)

    for s in range(s_loc):
        @pl.loop(0, nt // tile)
        def _(i):
            rows = lo[pl.ds(pl.multiple_of(s * nt + i * tile, tile), tile), :]
            update = lax.dot_general(
                rows, pivots, (((1,), (1,)), ((), ())), preferred_element_type=jnp.float32
            )
            acc[pl.ds(pl.multiple_of(i * tile, tile), tile), s * c:(s + 1) * c] = -update

    def arrive(j):
        for mask in range(nf - 1, 0, -1):
            arrival(j, mask).wait_recv()
        own_copy(j).wait()

    def term(j, i):
        rows = pl.ds(pl.multiple_of(i * tile, tile), tile)
        right = rbuf[j].reshape(cols, width)
        return acc[rows, :] + jnp.dot(table[j, rows, :], right, preferred_element_type=jnp.float32)

    @pl.loop(0, nch - 1)
    def _(j):
        arrive(j)

        @pl.loop(0, nt // tile)
        def _(i):
            acc[pl.ds(pl.multiple_of(i * tile, tile), tile), :] = term(j, i)

    last = nch - 1
    arrive(last)

    @pl.loop(0, nt // tile)
    def _(i):
        value = term(last, i).astype(jnp.bfloat16)
        for s in range(s_loc):
            out_ref[pl.ds(pl.multiple_of(s * nt + i * tile, tile), tile), :] = value[:, s * c:(s + 1) * c]

    @pl.loop(0, nch)
    def _(j):
        for mask in range(nf - 1, 0, -1):
            remote(j, mask).wait_send()

    for mask in range(1, ng):
        pivot_copy(mask, grp).wait_send()


def per_device(nf, ng, transfer, adjoint, lower_rows, pivot_store, owners, inverse_factor):
    kl, _, sl, m = transfer.shape
    c = adjoint.shape[3]
    kc = min(CHUNK, kl)
    nch = kl // kc
    s_loc = sl // nf
    rows = lower_rows.shape[0]
    nt = rows // s_loc
    bf16 = jnp.bfloat16
    reduced = pl.pallas_call(
        functools.partial(kernel, nf, ng, kc),
        out_shape=jax.ShapeDtypeStruct((rows, c), bf16),
        in_specs=[pl.BlockSpec(memory_space=pltpu.SMEM)] + [pl.BlockSpec(memory_space=pl.ANY)] * 4,
        out_specs=pl.BlockSpec(memory_space=pltpu.VMEM),
        scratch_shapes=[
            pltpu.VMEM(transfer.shape, bf16),
            pltpu.VMEM(adjoint.shape, bf16),
            pltpu.VMEM(lower_rows.shape, bf16),
            pltpu.VMEM((ng,) + pivot_store.shape, bf16),
            pltpu.VMEM((2, kc * sl, c), jnp.float32),
            pltpu.VMEM((nch, nf, 2 * kc, s_loc * c), bf16),
            pltpu.VMEM((nch, nf, 2 * kc, s_loc * c), bf16),
            pltpu.VMEM((nch, nt, nf * 2 * kc), bf16),
            pltpu.VMEM((nt, s_loc * c), jnp.float32),
            pltpu.SemaphoreType.DMA((nch, 2)),
            pltpu.SemaphoreType.DMA,
            pltpu.SemaphoreType.DMA,
            pltpu.SemaphoreType.DMA((nch,)),
            pltpu.SemaphoreType.DMA((nch, nf)),
            pltpu.SemaphoreType.DMA((nch, nf)),
            pltpu.SemaphoreType.DMA((ng,)),
            pltpu.SemaphoreType.DMA((ng,)),
        ],
        compiler_params=pltpu.CompilerParams(
            collective_id=0, has_side_effects=True, vmem_limit_bytes=52 * 1024 * 1024
        ),
    )(owners, transfer, adjoint, lower_rows, pivot_store)
    return jnp.dot(reduced, inverse_factor, preferred_element_type=jnp.float32).astype(bf16)


def solution(mesh):
    nf, ng = mesh.shape["freq"], mesh.shape["grp"]
    in_specs = (
        P("freq", None, "grp", None),
        P("freq", None, None, None),
        P(("grp", "freq"), None),
        P("grp", None),
        P(),
        P(),
    )
    out_specs = P(("grp", "freq"), None)
    return jax.shard_map(
        functools.partial(per_device, nf, ng),
        mesh=mesh, in_specs=in_specs, out_specs=out_specs, check_vma=False,
    )
```

time: 88.2 us -> 36.1 us (0.41)
  Pallas kernels: 0 us -> 32.9 us
  waiting for transfers between devices: 26.7 us -> 0 us
  matrix products: 20.4 us -> 1.39 us
  between operations: 13.5 us -> 0.02 us
  other arithmetic: 10.2 us -> 0 us
  local copies, waits for them, and re-layouts: 10.7 us -> 1.56 us
  starting transfers between devices: 6.39 us -> 0 us
    pallas_call x0 -> x1, Pallas kernels: none -> 32.9 us  [per_device(): pl.pallas_call(functools.partial(kernel, nf, ng, kc), out_shape=jax.Shape...]
    all_to_all x1 -> x0, waiting for transfers between devices: 16.4 us -> none  [per_device(): lax.all_to_all(spectra, 'freq', split_axis=1, concat_axis=0, tiled=True)]
    dot_general x5 -> x0, matrix products: 16.4 us -> none  [the longest x4 13.8 us: product(): jnp.einsum('ksm,kmc->ksc', left, right, preferred_element_type=jnp.float32)]
    psum x1 -> x0, waiting for transfers between devices: 10.3 us -> none  [per_device(): combined = lax.psum(local_blocks.astype(jnp.bfloat16), 'grp')]
    another operation x2 -> x0, other arithmetic: 9.42 us -> none
    all_to_all x1 -> x0, starting transfers between devices: 6.35 us -> none  [per_device(): lax.all_to_all(spectra, 'freq', split_axis=1, concat_axis=0, tiled=True)]
    transpose x1 -> x0, local copies, waits for them, and re-layouts: 2.91 us -> none  [per_device(): jnp.einsum('qtk,ksqc->stc', table, lax.all_to_all(spectra, 'freq', split_...]
    reshape x1 -> x0, local copies, waits for them, and re-layouts: 2.91 us -> none  [per_device(): hessian = hessian.reshape(-1, hessian.shape[-1])]
  transfers between devices with their start and end apart: 2 -> 0, of which waited for: 2 -> 0; matrix products, arithmetic and copies ran while one was open for 23% -> 0% of each run, Pallas kernels for 0% -> 0%
where the time goes in v1:
time: 36.1 us; the launch traced here: 35.9 us
  Pallas kernels  32.9 us (91%)
  local copies, waits for them, and re-layouts  1.56 us (4%)
  matrix products  1.39 us (4%)
    pallas_call x1, Pallas kernels, per_device(): pl.pallas_call(functools.partial(kernel, nf, ng, kc), out_shape=jax.Shape...  32.9 us
    unnamed x6, local copies, waits for them, and re-layouts  1.56 us
    dot_general x1, matrix products, per_device(): jnp.dot(reduced, inverse_factor, preferred_element_type=jnp.float32)  1.39 us

profile of v1, /device:TPU:0, one launch (start us, length us, event | category | flops | bytes accessed | tf_op | source)
XLA Modules:
  0.0 35.9 jit_solution(3505309188134022316)
XLA Ops:
  0.0 0.0 copy-start
  0.0 0.0 copy-start.1
  0.0 0.9 %copy-done.1 = bf16[128,384]{1,0:T(8,128)(2,1)S(1)} copy-done((bf16[128,384]{1,0:T(8,128)(2,1)S(1)}, bf16[128,384]{1,0:T(8,128)(2,1)}, u32[]{:S(2)}) %copy-start.1) | copy-done | bytes 98328
  0.9 0.0 copy-start.2
  0.9 0.7 %copy-done.2 = s32[3]{0:T(128)S(1)} copy-done((s32[3]{0:T(128)S(1)}, s32[3]{0:T(128)}, u32[]{:S(2)}) %copy-start.2) | copy-done | bytes 36
  1.6 32.9 %shard_map.64 = bf16[4096,128]{1,0:T(8,128)(2,1)S(1)} custom-call(s32[3]{0:T(128)S(1)} %copy-done.2, bf16[64,2,32,512]{3,2,1,0:T(8,128)(2,1)} %tr_hbm.1, bf16[64,2,512,128]{3,2,1,0:T(8,128)(2,1)} %ad_hbm.1, bf16[4096,384]{1,0:T(8,128)(2,1)} %lo_hbm.1, bf16[128,384]{1,0:T(8,128)(2,1)S(1)} %copy-done.1), custom_call_target="tpu_custom_call" | custom-call | tf_op jit(solution)/shard_map/pallas_call | solution.py:222
  34.5 0.0 copy-done
  34.5 1.4 %convolution_convert_fusion = bf16[4096,128]{1,0:T(8,128)(2,1)} fusion(bf16[4096,128]{1,0:T(8,128)(2,1)S(1)} %shard_map.64, bf16[128,128]{1,0:T(8,128)(2,1)S(1)} %copy-done), kind=kOutput, calls=%fused_computation | convolution fusion | flops 134742016 | bytes 2129920 | tf_op jit(solution)/shard_map/dot_general | solution.py:250
Async XLA Ops:
  0.0 34.5 %copy-start = (bf16[128,128]{1,0:T(8,128)(2,1)S(1)}, bf16[128,128]{1,0:T(8,128)(2,1)}, u32[]{:S(2)}) copy-start(bf16[128,128]{1,0:T(8,128)(2,1)} %param.11) | copy-start | bytes 98308
  0.0 0.9 %copy-start.1 = (bf16[128,384]{1,0:T(8,128)(2,1)S(1)}, bf16[128,384]{1,0:T(8,128)(2,1)}, u32[]{:S(2)}) copy-start(bf16[128,384]{1,0:T(8,128)(2,1)} %pv_hbm.1) | copy-start | bytes 294916
  0.9 0.7 %copy-start.2 = (s32[3]{0:T(128)S(1)}, s32[3]{0:T(128)}, u32[]{:S(2)}) copy-start(s32[3]{0:T(128)} %owners_ref.1) | copy-start | bytes 40

commit v2 on v1

--- a/solution.py
+++ b/solution.py
@@ -11,6 +11,9 @@
 MESH = pl.DeviceIdType.MESH
 CHUNK = 8
 AHEAD = 3
+TILE = 1024
+VMEM_BYTES = 64 * 1024 * 1024
+SPARE = 11 * 1024 * 1024
 COARSE = 32
 
 
@@ -26,9 +29,9 @@
 
 def kernel(
     nf, ng, kc,
-    owners_ref, tr_hbm, ad_hbm, lo_hbm, pv_hbm, out_ref,
-    tr, ad, lo, pv, spec, sbuf, rbuf, table, acc,
-    in_sem, lo_sem, pv_sem, own_sem, send_sem, recv_sem, psend_sem, precv_sem,
+    owners_hbm, tr_hbm, ad_hbm, lo_hbm, pv_hbm, out_ref,
+    owners, tr, ad, lo, pv, spec, sbuf, rbuf, table, acc,
+    in_sem, owners_sem, lo_sem, pv_sem, own_sem, send_sem, recv_sem, psend_sem, precv_sem,
 ):
     kl, _, sl, _ = tr.shape
     c = ad.shape[3]
@@ -38,12 +41,6 @@
     me = lax.axis_index("freq")
     grp = lax.axis_index("grp")
 
-    barrier = pltpu.get_barrier_semaphore()
-    for mask in range(1, nf):
-        pl.semaphore_signal(barrier, inc=1, device_id={"freq": flip(me, mask)}, device_id_type=MESH)
-    for mask in range(1, ng):
-        pl.semaphore_signal(barrier, inc=1, device_id={"grp": flip(grp, mask)}, device_id_type=MESH)
-
     def loads(j):
         rows = pl.ds(j * kc, kc)
         return (
@@ -52,15 +49,19 @@
         )
 
     lo_copy = pltpu.make_async_copy(lo_hbm, lo, lo_sem)
+    owners_copy = pltpu.make_async_copy(owners_hbm, owners, owners_sem)
     pv_copy = pltpu.make_async_copy(pv_hbm, pv.at[grp], pv_sem)
 
-    for j in range(min(AHEAD, nch)):
-        for copy in loads(j):
-            copy.start()
+    for copy in loads(0):
+        copy.start()
+
+    barrier = pltpu.get_barrier_semaphore()
+    for mask in range(1, nf):
+        pl.semaphore_signal(barrier, inc=1, device_id={"freq": flip(me, mask)}, device_id_type=MESH)
+    for mask in range(1, ng):
+        pl.semaphore_signal(barrier, inc=1, device_id={"grp": flip(grp, mask)}, device_id_type=MESH)
 
     def spectra(j):
-        for copy in loads(j):
-            copy.wait()
         for i in range(kc):
             k = j * kc + i
             right = jnp.concatenate([ad[k, 0], ad[k, 1]], axis=1)
@@ -108,14 +109,21 @@
             device_id_type=MESH,
         )
 
-    def send(j):
-        for mask in range(nf - 1, 0, -1):
+    far = tuple(range(nf - 1, nf // 2 - 1, -1))
+    near = tuple(range(nf // 2 - 1, 0, -1))
+    def send(j, masks):
+        for mask in masks:
             remote(j, mask).start()
         own_copy(j).start()
 
+    for copy in loads(0):
+        copy.wait()
+    for j in range(1, min(AHEAD, nch)):
+        for copy in loads(j):
+            copy.start()
     spectra(0)
     pl.semaphore_wait(barrier, nf - 1 + ng - 1)
-    send(0)
+    send(0, far + near)
 
     @pl.loop(1, nch)
     def _(j):
@@ -124,9 +132,12 @@
             for copy in loads(j + AHEAD - 1):
                 copy.start()
 
+        for copy in loads(j):
+            copy.wait()
         spectra(j)
-        send(j)
-
+        send(j, near + far)
+
+    owners_copy.start()
     pv_copy.start()
     lo_copy.start()
     for mask in range(1, ng):
@@ -156,14 +167,15 @@
             table[j, a * COARSE:(a + 1) * COARSE, :] = value.astype(jnp.bfloat16)
 
     lo_copy.wait()
+    owners_copy.wait()
     pv_copy.wait()
     for mask in range(1, ng):
         pivot_copy(mask, flip(grp, mask)).wait_recv()
     panels = lo.shape[1] // c
     pivots = jnp.concatenate(
-        [pv[owners_ref[p], :, p * c:(p + 1) * c] for p in range(panels)], axis=1
+        [pv[owners[p], :, p * c:(p + 1) * c] for p in range(panels)], axis=1
     )
-    tile = min(256, nt)
+    tile = min(TILE, nt)
 
     for s in range(s_loc):
         @pl.loop(0, nt // tile)
@@ -219,12 +231,14 @@
     rows = lower_rows.shape[0]
     nt = rows // s_loc
     bf16 = jnp.bfloat16
+    in_hbm = lambda x: pltpu.with_memory_space_constraint(x, pltpu.HBM)
     reduced = pl.pallas_call(
         functools.partial(kernel, nf, ng, kc),
         out_shape=jax.ShapeDtypeStruct((rows, c), bf16),
-        in_specs=[pl.BlockSpec(memory_space=pltpu.SMEM)] + [pl.BlockSpec(memory_space=pl.ANY)] * 4,
+        in_specs=[pl.BlockSpec(memory_space=pltpu.HBM)] * 5,
         out_specs=pl.BlockSpec(memory_space=pltpu.VMEM),
         scratch_shapes=[
+            pltpu.SMEM(owners.shape, jnp.int32),
             pltpu.VMEM(transfer.shape, bf16),
             pltpu.VMEM(adjoint.shape, bf16),
             pltpu.VMEM(lower_rows.shape, bf16),
@@ -237,6 +251,7 @@
             pltpu.SemaphoreType.DMA((nch, 2)),
             pltpu.SemaphoreType.DMA,
             pltpu.SemaphoreType.DMA,
+            pltpu.SemaphoreType.DMA,
             pltpu.SemaphoreType.DMA((nch,)),
             pltpu.SemaphoreType.DMA((nch, nf)),
             pltpu.SemaphoreType.DMA((nch, nf)),
@@ -244,9 +259,9 @@
             pltpu.SemaphoreType.DMA((ng,)),
         ],
         compiler_params=pltpu.CompilerParams(
-            collective_id=0, has_side_effects=True, vmem_limit_bytes=52 * 1024 * 1024
+            collective_id=0, has_side_effects=True, vmem_limit_bytes=VMEM_BYTES - 2 * rows * c - SPARE
         ),
-    )(owners, transfer, adjoint, lower_rows, pivot_store)
+    )(in_hbm(owners), transfer, adjoint, lower_rows, in_hbm(pivot_store))
     return jnp.dot(reduced, inverse_factor, preferred_element_type=jnp.float32).astype(bf16)
 
 

time: 36.1 us -> 33.5 us (0.928)
  local copies, waits for them, and re-layouts: 1.56 us -> 0.01 us
  Pallas kernels: 32.9 us -> 31.9 us
    unnamed x6 -> x2, local copies, waits for them, and re-layouts: 1.56 us -> 0.01 us
    pallas_call x1, Pallas kernels: 32.9 us -> 31.9 us  [per_device(): pl.pallas_call(functools.partial(kernel, nf, ng, kc), out_shape=jax.Shape...]
where the time goes in v2:
time: 33.5 us; the launch traced here: 33.3 us
  Pallas kernels  31.9 us (95%)
  matrix products  1.39 us (4%)
    pallas_call x1, Pallas kernels, per_device(): pl.pallas_call(functools.partial(kernel, nf, ng, kc), out_shape=jax.Shape...  31.9 us
    dot_general x1, matrix products, per_device(): jnp.dot(reduced, inverse_factor, preferred_element_type=jnp.float32)  1.39 us

profile of v2, /device:TPU:0, one launch (start us, length us, event | category | flops | bytes accessed | tf_op | source)
XLA Modules:
  0.0 33.3 jit_solution(2269274423763961719)
XLA Ops:
  0.0 0.0 copy-start
  0.0 31.9 %shard_map.64 = bf16[4096,128]{1,0:T(8,128)(2,1)S(1)} custom-call(s32[3]{0:T(128)} %owners_hbm.1, bf16[64,2,32,512]{3,2,1,0:T(8,128)(2,1)} %tr_hbm.1, bf16[64,2,512,128]{3,2,1,0:T(8,128)(2,1)} %ad_hbm.1, bf16[4096,384]{1,0:T(8,128)(2,1)} %lo_hbm.1, bf16[128,384]{1,0:T(8,128)(2,1)} %pv_hbm.1), custom_call_target="tpu_custom_call" | custom-call | tf_op jit(solution)/shard_map/pallas_call | solution.py:235
  31.9 0.0 copy-done
  31.9 1.4 %convolution_convert_fusion = bf16[4096,128]{1,0:T(8,128)(2,1)} fusion(bf16[4096,128]{1,0:T(8,128)(2,1)S(1)} %shard_map.64, bf16[128,128]{1,0:T(8,128)(2,1)S(1)} %copy-done), kind=kOutput, calls=%fused_computation | convolution fusion | flops 134742016 | bytes 2129920 | tf_op jit(solution)/shard_map/dot_general | solution.py:265
Async XLA Ops:
  0.0 31.9 %copy-start = (bf16[128,128]{1,0:T(8,128)(2,1)S(1)}, bf16[128,128]{1,0:T(8,128)(2,1)}, u32[]{:S(2)}) copy-start(bf16[128,128]{1,0:T(8,128)(2,1)} %param.11) | copy-start | bytes 98308
